TPU v7x, 32 devices: a whole 2x2x4 slice. The times are simulated.
32 devices in a mesh: ctx: 16 (over z, y, core), grp: 2 (over x).
Axes of the slice: x: 2, y: 2, z: 4, core: 2. Of those that a mesh axis runs over, the one named last changes fastest.
Arguments:
- query_in: bfloat16 [2560, 768], P(('grp', 'ctx')), parts along dimension 0, may hold values from -30 to 30
- key_in: bfloat16 [2560, 768], P(('grp', 'ctx')), parts along dimension 0, may hold values from -6 to 6
- value_in: bfloat16 [2560, 768], P(('grp', 'ctx')), parts along dimension 0, may hold values from -6 to 6
- length: int32 [2], P('grp'), parts along dimension 0, may hold values from 320 to 1280
- out_weight: bfloat16 [768, 1536], replicated, may hold values from -0.21875 to 0.21875
Outputs:
- projected: bfloat16 [2560, 1536], P(('grp', 'ctx')), parts along dimension 0
There are 2 independent parts, one for each index of `grp`. A program takes and returns all parts, laid end to end along the dimension named above; an argument that names none is the same for every part. Nothing has to cross between parts.
All inputs are finite; a program needn't handle non-finite values.
Results may differ from a plain program's by a relative error of at most 0.007.
Values may be sent and summed in bfloat16 or wider, within the bound.
A program may use at most 64 MiB of HBM per device.

v0:
```python
import jax
import jax.numpy as jnp
from jax import lax
from jax.sharding import PartitionSpec as P

HEADS = 12
HDIM = 64


def body(query_in, key_in, value_in, length, out_weight):
    local_rows = query_in.shape[0]
    offset = lax.axis_index("ctx") * local_rows
    valid_len = length[0]
    score_scale = 1.0 / jnp.sqrt(jnp.float32(HDIM))
    query_heads = query_in.reshape(local_rows, HEADS, HDIM).transpose(1, 0, 2)
    start_state = (
        jnp.full((HEADS, local_rows), -1e30, jnp.float32),
        jnp.zeros((HEADS, local_rows), jnp.float32),
        jnp.zeros((HEADS, local_rows, HDIM), jnp.float32),
    )
    key_part = lax.all_gather(key_in, "ctx", axis=0, tiled=True)
    value_part = lax.all_gather(value_in, "ctx", axis=0, tiled=True)
    part_rows = key_part.shape[0]
    key_live = (jnp.arange(part_rows, dtype=jnp.int32) < valid_len)[None, :]
    key_heads = key_part.reshape(part_rows, HEADS, HDIM).transpose(1, 0, 2)
    value_heads = value_part.reshape(part_rows, HEADS, HDIM).transpose(1, 0, 2)

    def fold_head(operands):
        query_h, key_h, value_h, run_max, run_sum, run_acc = operands
        scores = jnp.dot(query_h, key_h.T, preferred_element_type=jnp.float32) * score_scale
        new_max = jnp.maximum(
            run_max, jnp.max(jnp.where(key_live, scores, jnp.float32(-1e30)), axis=1)
        )
        expons = jnp.where(key_live, jnp.exp(scores - new_max[:, None]), jnp.float32(0.0))
        factor = jnp.exp(run_max - new_max)
        added = jnp.dot(expons.astype(jnp.bfloat16), value_h, preferred_element_type=jnp.float32)
        return (
            new_max,
            run_sum * factor + jnp.sum(expons, axis=1),
            run_acc * factor[:, None] + added,
        )

    running, denominator, weighted = lax.map(
        fold_head, (query_heads, key_heads, value_heads) + tuple(start_state)
    )
    heads_out = (
        (weighted / denominator[:, :, None]).transpose(1, 0, 2).reshape(local_rows, HEADS * HDIM)
    )
    query_live = offset + jnp.arange(local_rows, dtype=jnp.int32) < valid_len
    attended = jnp.where(query_live[:, None], heads_out, jnp.float32(0.0)).astype(jnp.bfloat16)
    return jnp.dot(attended, out_weight, preferred_element_type=jnp.float32).astype(jnp.bfloat16)


def solution(mesh):
    in_specs = (
        P(("grp", "ctx"), None),
        P(("grp", "ctx"), None),
        P(("grp", "ctx"), None),
        P("grp"),
        P(),
    )
    out_specs = P(("grp", "ctx"), None)
    return jax.shard_map(body, mesh=mesh, in_specs=in_specs, out_specs=out_specs, check_vma=False)
```

profile of v0, /device:TPU:0, one launch (start us, length us, event | category | flops | bytes accessed | tf_op | source)
XLA Modules:
  0.0 149.1 jit_solution(4521468957374590369)
XLA Ops:
  6.5 0.7 all-gather.3.cloned.1.call-update
  7.3 0.7 all-gather.5.cloned.1.call-update
  8.0 1.1 copy.12
  9.8 43.4 %all-gather.3.cloned.1.call-done = bf16[1280,768]{1,0:T(8,128)(2,1)} async-done(((bf16[80,768]{1,0:T(8,128)(2,1)}), bf16[1280,768]{1,0:T(8,128)(2,1)}) %all-gather.3.cloned.1.call-update) | async-done | bytes 1966096 | tf_op jit(solution)/shard_map/all_gather | solution.py:21
  53.2 4.0 %copy.13 = bf16[1280,768]{0,1:T(8,128)(2,1)} copy(bf16[1280,768]{1,0:T(8,128)(2,1)} %all-gather.3.cloned.1.call-done) | data formatting | bytes 3932160 | tf_op jit(solution)/shard_map/all_gather | solution.py:21
  57.2 38.1 %all-gather.5.cloned.1.call-done = bf16[1280,768]{1,0:T(8,128)(2,1)} async-done(((bf16[80,768]{1,0:T(8,128)(2,1)}), bf16[1280,768]{1,0:T(8,128)(2,1)}) %all-gather.5.cloned.1.call-update) | async-done | bytes 1966096 | tf_op jit(solution)/shard_map/all_gather | solution.py:22
  95.3 4.0 %copy.14 = bf16[1280,768]{0,1:T(8,128)(2,1)} copy(bf16[1280,768]{1,0:T(8,128)(2,1)} %all-gather.5.cloned.1.call-done) | data formatting | bytes 3932160 | tf_op jit(solution)/shard_map/all_gather | solution.py:22
  99.3 41.6 %while.13 = (s32[]{:T(128)}, f32[12,80]{1,0:T(8,128)S(1)}, f32[12,80,64]{1,2,0:T(8,128)S(1)}, bf16[12,80,64]{1,2,0:T(8,128)(2,1)S(1)}, bf16[12,1280,64]{1,2,0:T(...) while((s32[]{:T(128)}, f32[12,80]{1,0:T(8,128)S(1)}, ...), condition=%wide.region_3.4_spmd.clone, body=%wide.region_0.3_spmd.clone.sunk | while | flops 27142640 | bytes 1618981 | solution.py:43
  99.3 0.7 compare_reduce_fusion.2
  100.0 1.3 select_reduce_fusion.2
  101.5 1.2 fusion.29
  102.7 0.7 compare_reduce_fusion.2
  103.4 1.3 select_reduce_fusion.2
  104.7 0.2 fusion.28
  105.0 1.2 fusion.29
  106.2 0.7 compare_reduce_fusion.2
  106.9 1.3 select_reduce_fusion.2
  108.4 1.2 fusion.29
  109.7 0.7 compare_reduce_fusion.2
  110.4 1.3 select_reduce_fusion.2
  111.9 1.2 fusion.29
  113.2 0.7 compare_reduce_fusion.2
  113.8 1.3 select_reduce_fusion.2
  115.1 0.2 fusion.28
  115.4 1.2 fusion.29
  116.6 0.7 compare_reduce_fusion.2
  117.3 1.3 select_reduce_fusion.2
  118.8 1.2 fusion.29
  120.1 0.7 compare_reduce_fusion.2
  120.8 1.3 select_reduce_fusion.2
  122.3 1.2 fusion.29
  123.6 0.7 compare_reduce_fusion.2
  124.2 1.3 select_reduce_fusion.2
  125.5 0.2 fusion.28
  125.8 1.2 fusion.29
  127.0 0.7 compare_reduce_fusion.2
  127.7 1.3 select_reduce_fusion.2
  129.2 1.2 fusion.29
  130.5 0.7 compare_reduce_fusion.2
  131.2 1.3 select_reduce_fusion.2
  132.7 1.2 fusion.29
  134.0 0.7 compare_reduce_fusion.2
  134.7 1.3 select_reduce_fusion.2
  136.2 1.2 fusion.29
  137.4 0.7 compare_reduce_fusion.2
  138.1 1.3 select_reduce_fusion.2
  139.7 1.2 fusion.29
  141.0 1.3 convolution_convert_fusion
  (54 shorter events, 2.9 us)
Async XLA Ops:
  6.5 134.5 %copy-start = (bf16[768,1536]{1,0:T(8,128)(2,1)S(1)}, bf16[768,1536]{1,0:T(8,128)(2,1)}, u32[]{:S(2)}) copy-start(bf16[768,1536]{1,0:T(8,128)(2,1)} %param.11) | copy-start | bytes 7077892
  6.5 46.7 %all-gather.3.cloned.1.call-start = ((), (), s32[]{:S(2)}) async-start(), calls=%async_computation | async-start | bytes 2088960 | tf_op jit(solution)/shard_map/all_gather | solution.py:21
  7.3 88.0 %all-gather.5.cloned.1.call-start = ((), (), s32[]{:S(2)}) async-start(), calls=%async_computation.1 | async-start | bytes 2088960 | tf_op jit(solution)/shard_map/all_gather | solution.py:22
Sparse Core Ops, SparseCore 0:
  9.6 43.5 all-gather.2
  55.5 39.7 all-gather.4
where the time goes:
time: 150 us; the launch traced here: 149 us
  waiting for transfers between devices  82.9 us (55%)
  matrix products  30.9 us (21%)
  between operations  14.1 us (9%)
  other arithmetic  11.3 us (8%)
  local copies, waits for them, and re-layouts  9.49 us (6%)
    all_gather x1, waiting for transfers between devices, body(): key_part = lax.all_gather(key_in, 'ctx', axis=0, tiled=True)  43.4 us
    all_gather x1, waiting for transfers between devices, body(): value_part = lax.all_gather(value_in, 'ctx', axis=0, tiled=True)  38.1 us
    dot_general x12, matrix products, fold_head(): jnp.dot(query_h, key_h.T, preferred_element_type=jnp.float32) * score_scale  15.2 us
    dot_general x12, matrix products, fold_head(): jnp.dot(expons.astype(jnp.bfloat16), value_h, preferred_element_type=jnp....  14.4 us
    lt x12, other arithmetic, body(): key_live = (jnp.arange(part_rows, dtype=jnp.int32) < valid_len)[None, :]  8.16 us
    all_gather x1, local copies, waits for them, and re-layouts, body(): value_part = lax.all_gather(value_in, 'ctx', axis=0, tiled=True)  4 us
    all_gather x1, local copies, waits for them, and re-layouts, body(): key_part = lax.all_gather(key_in, 'ctx', axis=0, tiled=True)  3.97 us
  transfers between devices with their start and end apart: 2, of which 2 were waited for; matrix products, arithmetic and copies ran while one was open for 3% of the time, Pallas kernels for 0%

commit v1 on v0

v1 whole, which is shorter than its diff:
```python
import functools

import jax
import jax.numpy as jnp
from jax import lax
from jax.experimental import pallas as pl
from jax.experimental.pallas import tpu as pltpu
from jax.sharding import PartitionSpec as P

HEADS = 12
HDIM = 64
LEVELS = 4
MESH = pl.DeviceIdType.MESH
NT = (((1,), (1,)), ((), ()))


def kernel(
    n, q_ref, k_ref, v_ref, len_ref, w_hbm, out_ref,
    send_q, send_k, send_v, q_buf, k_buf, v_buf, o_send, o_buf, w_buf,
    w_sem, sq_sem, rq_sem, sk_sem, rk_sem, sv_sem, rv_sem, so_sem, ro_sem,
):
    rows = q_ref.shape[0]
    cols = n // LEVELS
    chips = cols // 2
    me = lax.axis_index("ctx")
    level, col = me // cols, me % cols
    core = col % 2
    sibling = level * cols + col + 1 - 2 * core

    def mate(off):
        return ((level + off) % LEVELS) * cols + col

    def chip_col(off):
        return (col + 2 * off) % cols

    w_copy = pltpu.make_async_copy(w_hbm, w_buf, w_sem)
    w_copy.start()

    barrier = pltpu.get_barrier_semaphore()
    greeted = [mate(off) for off in range(1, LEVELS)] + [sibling]
    greeted += [level * cols + chip_col(off) for off in range(1, chips)]
    for other in greeted:
        pl.semaphore_signal(barrier, inc=1, device_id={"ctx": other}, device_id_type=MESH)

    scale = jnp.asarray(HDIM ** -0.5, jnp.bfloat16)
    for d in range(LEVELS):
        pair = slice(128 * d, 128 * d + 128)
        one = slice(512 + 64 * d, 576 + 64 * d)
        send_k[d, :, :128] = k_ref[:, pair]
        send_k[d, :, 128:] = jnp.concatenate([k_ref[:, one], v_ref[:, one]], axis=1)
        send_q[d, :, :128] = q_ref[:, pair] * scale
        q_one = q_ref[:, one] * scale
        send_q[d, :, 128:] = jnp.concatenate([q_one, jnp.zeros_like(q_one)], axis=1)
        send_v[d] = v_ref[:, pair]
    k_buf[me] = send_k[level]
    v_buf[me] = send_v[level]
    q_buf[level] = send_q[level]

    pl.semaphore_wait(barrier, len(greeted))

    sent = []

    def remote(src, dst, send_sem, recv_sem, target):
        copy = pltpu.make_async_remote_copy(
            src_ref=src, dst_ref=dst, send_sem=send_sem, recv_sem=recv_sem,
            device_id={"ctx": target}, device_id_type=MESH,
        )
        copy.start()
        sent.append(copy)

    def arrived(buf, slot, sem):
        pltpu.make_async_remote_copy(
            src_ref=buf.at[slot], dst_ref=buf.at[slot], send_sem=sem.at[slot], recv_sem=sem.at[slot],
            device_id={"ctx": sibling}, device_id_type=MESH,
        ).wait_recv()

    used = {"k": 0, "v": 0}

    def forward(kind, slot, target):
        buf, send, recv = (k_buf, sk_sem, rk_sem) if kind == "k" else (v_buf, sv_sem, rv_sem)
        remote(buf.at[slot], buf.at[slot], send.at[used[kind]], recv.at[slot], target)
        used[kind] += 1

    def phase_one(kind, off):
        buf, src, send, recv = (
            (k_buf, send_k, sk_sem, rk_sem) if kind == "k" else (v_buf, send_v, sv_sem, rv_sem)
        )
        other = (level + off) % LEVELS
        remote(src.at[other], buf.at[me], send.at[used[kind]], recv.at[me], mate(off))
        used[kind] += 1

    def spread(kind, slot):
        for off in range(1, chips):
            forward(kind, slot, level * cols + chip_col(off))
        forward(kind, slot, sibling)

    order = (2, 1, 3)
    for off in order:
        other = (level + off) % LEVELS
        phase_one("k", off)
        remote(send_q.at[other], q_buf.at[level], sq_sem.at[off], rq_sem.at[level], mate(off))
    spread("k", me)
    for off in order:
        phase_one("v", off)
    spread("v", me)

    def source(off):
        return (level - off + LEVELS) % LEVELS

    buffers = {"k": (k_buf, rk_sem), "v": (v_buf, rv_sem)}
    for kind in ("k", "v"):
        buf, sem = buffers[kind]
        for off in (0,) + order:
            if off:
                slot = source(off) * cols + col
                arrived(buf, slot, sem)
                spread(kind, slot)
        for off in (0,) + order:
            for hop in range(1, chips):
                slot = source(off) * cols + chip_col(hop)
                arrived(buf, slot, sem)
                forward(kind, slot, sibling)
    for kind in ("k", "v"):
        buf, sem = buffers[kind]
        for off in (0,) + order:
            for hop in range(chips):
                arrived(buf, source(off) * cols + chip_col(hop) + 1 - 2 * core, sem)
    for off in order:
        arrived(q_buf, source(off), rq_sem)

    valid = len_ref[0]
    frames = n * rows
    live = lax.broadcasted_iota(jnp.int32, (1, frames), 1) < valid
    low = lax.broadcasted_iota(jnp.int32, (1, 128), 1) < HDIM
    k_pair = k_buf[:, :, :128].reshape(frames, 128)
    kv_one = k_buf[:, :, 128:].reshape(frames, 128)
    v_pair = v_buf[...].reshape(frames, 128)

    def attend(q, k, v):
        s = lax.dot_general(q, k, NT, preferred_element_type=jnp.float32)
        s = jnp.where(live, s, jnp.float32(-1e30))
        e = jnp.exp(s - jnp.max(s, axis=1, keepdims=True))
        total = jnp.sum(e, axis=1, keepdims=True)
        return jnp.dot(e.astype(jnp.bfloat16), v, preferred_element_type=jnp.float32) / total

    for off in order + (0,):
        j = (level + off) % LEVELS
        q_pair = q_buf[j, :, :128]
        zero = jnp.zeros_like(q_pair)
        q_two = jnp.concatenate([jnp.where(low, q_pair, zero), jnp.where(low, zero, q_pair)], axis=0)
        o_two = attend(q_two, k_pair, v_pair)
        o_one = attend(q_buf[j, :, 128:], kv_one, kv_one)
        row = (j * cols + col) * rows + lax.broadcasted_iota(jnp.int32, (rows, 1), 0)
        keep = row < valid
        none = jnp.float32(0.0)
        o_pair = jnp.where(keep, jnp.where(low, o_two[:rows], o_two[rows:]), none).astype(jnp.bfloat16)
        o_one = jnp.where(keep, o_one, none).astype(jnp.bfloat16)
        if off:
            o_send[off - 1, :, :128] = o_pair
            o_send[off - 1, :, 128:] = o_one
            remote(o_send.at[off - 1], o_buf.at[level], so_sem.at[off - 1], ro_sem.at[level], mate(off))
        else:
            o_buf[level, :, :128] = o_pair
            o_buf[level, :, 128:] = o_one

    for off in order:
        arrived(o_buf, source(off), ro_sem)
    parts = [o_buf[g, :, :128] for g in range(LEVELS)]
    for g in range(0, LEVELS, 2):
        parts.append(
            jnp.concatenate([o_buf[g, :, 192:], o_buf[g + 1, :, 192:]], axis=1)
        )
    w_copy.wait()
    attended = jnp.concatenate(parts, axis=1)
    out_ref[...] = jnp.dot(attended, w_buf[...], preferred_element_type=jnp.float32).astype(jnp.bfloat16)
    for copy in sent:
        copy.wait_send()


def body(n, query_in, key_in, value_in, length, out_weight):
    rows, cin = query_in.shape
    width = out_weight.shape[1]
    bf = jnp.bfloat16
    chips = n // LEVELS // 2
    copies = (LEVELS - 1) + LEVELS * chips + LEVELS * (chips - 1)
    dma = pltpu.SemaphoreType.DMA
    vmem = pl.BlockSpec(memory_space=pltpu.VMEM)
    return pl.pallas_call(
        functools.partial(kernel, n),
        out_shape=jax.ShapeDtypeStruct((rows, width), bf),
        in_specs=[vmem, vmem, vmem, pl.BlockSpec(memory_space=pltpu.SMEM), pl.BlockSpec(memory_space=pl.ANY)],
        out_specs=vmem,
        scratch_shapes=[
            pltpu.VMEM((LEVELS, rows, 256), bf),
            pltpu.VMEM((LEVELS, rows, 256), bf),
            pltpu.VMEM((LEVELS, rows, 128), bf),
            pltpu.VMEM((LEVELS, rows, 256), bf),
            pltpu.VMEM((n, rows, 256), bf),
            pltpu.VMEM((n, rows, 128), bf),
            pltpu.VMEM((LEVELS - 1, rows, 256), bf),
            pltpu.VMEM((LEVELS, rows, 256), bf),
            pltpu.VMEM((cin, width), bf),
            dma,
            dma((LEVELS,)),
            dma((LEVELS,)),
            dma((copies,)),
            dma((n,)),
            dma((copies,)),
            dma((n,)),
            dma((LEVELS,)),
            dma((LEVELS,)),
        ],
        compiler_params=pltpu.CompilerParams(
            collective_id=0, has_side_effects=True, vmem_limit_bytes=48 * 2**20
        ),
        name="attention",
    )(query_in, key_in, value_in, length, out_weight)


def solution(mesh):
    split = P(("grp", "ctx"), None)
    return jax.shard_map(
        functools.partial(body, mesh.shape["ctx"]),
        mesh=mesh,
        in_specs=(split, split, split, P("grp"), P()),
        out_specs=split,
        check_vma=False,
    )
```

time: 150 us -> 34.8 us (0.23)
  waiting for transfers between devices: 82.9 us -> 0 us
  matrix products: 30.9 us -> 0 us
  Pallas kernels: 0 us -> 28.9 us
  between operations: 14.1 us -> 0.67 us
  other arithmetic: 11.3 us -> 0 us
  local copies, waits for them, and re-layouts: 9.49 us -> 5.06 us
    all_gather x2 -> x0, waiting for transfers between devices: 81.5 us -> none  [the longest x1 43.4 us: body(): key_part = lax.all_gather(key_in, 'ctx', axis=0, tiled=True)]
    dot_general x25 -> x0, matrix products: 30.9 us -> none  [the longest x12 15.2 us: fold_head(): jnp.dot(query_h, key_h.T, preferred_element_type=jnp.float32) * score_scale]
    pallas_call x0 -> x1, Pallas kernels: none -> 28.9 us  [body(): pl.pallas_call(functools.partial(kernel, n), out_shape=jax.ShapeDtypeStru...]
    lt x13 -> x0, other arithmetic: 8.16 us -> none  [the longest x12 8.16 us: body(): key_live = (jnp.arange(part_rows, dtype=jnp.int32) < valid_len)[None, :]]
    all_gather x2 -> x0, local copies, waits for them, and re-layouts: 7.96 us -> none  [the longest x1 4 us: body(): value_part = lax.all_gather(value_in, 'ctx', axis=0, tiled=True)]
    unnamed x3 -> x9, local copies, waits for them, and re-layouts: 1.07 us -> 5.06 us
    reduce_sum x12 -> x0, other arithmetic: 2.83 us -> none  [fold_head(): jnp.sum(expons, axis=1)]
  transfers between devices with their start and end apart: 2 -> 0, of which waited for: 2 -> 0; matrix products, arithmetic and copies ran while one was open for 3% -> 0% of each run, Pallas kernels for 0% -> 0%
where the time goes in v1:
time: 34.8 us; the launch traced here: 34.6 us
  Pallas kernels  28.9 us (83%)
  local copies, waits for them, and re-layouts  5.06 us (15%)
  between operations  0.67 us (2%)
    pallas_call x1, Pallas kernels, body(): pl.pallas_call(functools.partial(kernel, n), out_shape=jax.ShapeDtypeStru...  28.9 us
    unnamed x9, local copies, waits for them, and re-layouts  5.06 us

profile of v1, /device:TPU:0, one launch (start us, length us, event | category | flops | bytes accessed | tf_op | source)
XLA Modules:
  0.0 34.6 jit_solution(14578082419426642822)
XLA Ops:
  0.7 0.0 copy-start
  0.7 1.7 %copy-done = bf16[768,1536]{1,0:T(8,128)(2,1)S(1)} copy-done((bf16[768,1536]{1,0:T(8,128)(2,1)S(1)}, bf16[768,1536]{1,0:T(8,128)(2,1)}, u32[]{:S(2)}) %copy-start) | copy-done | bytes 2359320
  2.3 0.0 copy-start.1
  2.3 0.9 %copy-done.1 = bf16[80,768]{1,0:T(8,128)(2,1)S(1)} copy-done((bf16[80,768]{1,0:T(8,128)(2,1)S(1)}, bf16[80,768]{1,0:T(8,128)(2,1)}, u32[]{:S(2)}) %copy-start.1) | copy-done | bytes 122904
  3.2 0.0 copy-start.2
  3.2 0.9 %copy-done.2 = bf16[80,768]{1,0:T(8,128)(2,1)S(1)} copy-done((bf16[80,768]{1,0:T(8,128)(2,1)S(1)}, bf16[80,768]{1,0:T(8,128)(2,1)}, u32[]{:S(2)}) %copy-start.2) | copy-done | bytes 122904
  4.1 0.0 copy-start.3
  4.1 0.9 %copy-done.3 = bf16[80,768]{1,0:T(8,128)(2,1)S(1)} copy-done((bf16[80,768]{1,0:T(8,128)(2,1)S(1)}, bf16[80,768]{1,0:T(8,128)(2,1)}, u32[]{:S(2)}) %copy-start.3) | copy-done | bytes 122904
  5.0 28.9 %attention.1 = bf16[80,1536]{1,0:T(8,128)(2,1)S(1)} custom-call(bf16[80,768]{1,0:T(8,128)(2,1)S(1)} %copy-done.1, bf16[80,768]{1,0:T(8,128)(2,1)S(1)} %copy-done.2, bf16[80,768]{1,0:T(8,128)(2,1)S(1)} %copy-done.3, s32[1]{0:T(128)S(6)} %copy.7.len_ref, bf16[768,1536]{1,0:T(8,128)(2,1)S(1)} %copy-done), custom_call_target="tpu_custom_call" | custom-call | tf_op jit(solution)/shard_map/attention/pallas_call | solution.py:188
  33.9 0.7 %copy.8 = bf16[80,1536]{1,0:T(8,128)(2,1)} copy(bf16[80,1536]{1,0:T(8,128)(2,1)S(1)} %attention.1) | data formatting | bytes 491520
Async XLA Ops:
  0.7 1.7 %copy-start = (bf16[768,1536]{1,0:T(8,128)(2,1)S(1)}, bf16[768,1536]{1,0:T(8,128)(2,1)}, u32[]{:S(2)}) copy-start(bf16[768,1536]{1,0:T(8,128)(2,1)} %w_hbm.1) | copy-start | bytes 7077892
  2.3 0.9 %copy-start.1 = (bf16[80,768]{1,0:T(8,128)(2,1)S(1)}, bf16[80,768]{1,0:T(8,128)(2,1)}, u32[]{:S(2)}) copy-start(bf16[80,768]{1,0:T(8,128)(2,1)} %q_ref.1) | copy-start | bytes 368644
  3.2 0.9 %copy-start.2 = (bf16[80,768]{1,0:T(8,128)(2,1)S(1)}, bf16[80,768]{1,0:T(8,128)(2,1)}, u32[]{:S(2)}) copy-start(bf16[80,768]{1,0:T(8,128)(2,1)} %k_ref.1) | copy-start | bytes 368644
  4.1 0.9 %copy-start.3 = (bf16[80,768]{1,0:T(8,128)(2,1)S(1)}, bf16[80,768]{1,0:T(8,128)(2,1)}, u32[]{:S(2)}) copy-start(bf16[80,768]{1,0:T(8,128)(2,1)} %v_ref.1) | copy-start | bytes 368644

commit v2 on v1

--- a/solution.py
+++ b/solution.py
@@ -15,9 +15,9 @@
 
 
 def kernel(
-    n, q_ref, k_ref, v_ref, len_ref, w_hbm, out_ref,
-    send_q, send_k, send_v, q_buf, k_buf, v_buf, o_send, o_buf, w_buf,
-    w_sem, sq_sem, rq_sem, sk_sem, rk_sem, sv_sem, rv_sem, so_sem, ro_sem,
+    n, q_hbm, k_hbm, v_hbm, len_ref, w_hbm, out_ref,
+    q_ref, k_ref, v_ref, send_q, send_k, send_v, q_buf, k_buf, v_buf, o_send, o_buf, w_buf,
+    in_sem, w_sem, sq_sem, rq_sem, sk_sem, rk_sem, sv_sem, rv_sem, so_sem, ro_sem,
 ):
     rows = q_ref.shape[0]
     cols = n // LEVELS
@@ -33,6 +33,12 @@
     def chip_col(off):
         return (col + 2 * off) % cols
 
+    loads = [
+        pltpu.make_async_copy(src, dst, in_sem.at[i])
+        for i, (src, dst) in enumerate(((k_hbm, k_ref), (q_hbm, q_ref), (v_hbm, v_ref)))
+    ]
+    for load in loads:
+        load.start()
     w_copy = pltpu.make_async_copy(w_hbm, w_buf, w_sem)
     w_copy.start()
 
@@ -41,6 +47,9 @@
     greeted += [level * cols + chip_col(off) for off in range(1, chips)]
     for other in greeted:
         pl.semaphore_signal(barrier, inc=1, device_id={"ctx": other}, device_id_type=MESH)
+
+    for load in loads:
+        load.wait()
 
     scale = jnp.asarray(HDIM ** -0.5, jnp.bfloat16)
     for d in range(LEVELS):
@@ -185,12 +194,16 @@
     copies = (LEVELS - 1) + LEVELS * chips + LEVELS * (chips - 1)
     dma = pltpu.SemaphoreType.DMA
     vmem = pl.BlockSpec(memory_space=pltpu.VMEM)
+    hbm = pl.BlockSpec(memory_space=pl.ANY)
     return pl.pallas_call(
         functools.partial(kernel, n),
         out_shape=jax.ShapeDtypeStruct((rows, width), bf),
-        in_specs=[vmem, vmem, vmem, pl.BlockSpec(memory_space=pltpu.SMEM), pl.BlockSpec(memory_space=pl.ANY)],
+        in_specs=[hbm, hbm, hbm, pl.BlockSpec(memory_space=pltpu.SMEM), hbm],
         out_specs=vmem,
         scratch_shapes=[
+            pltpu.VMEM((rows, cin), bf),
+            pltpu.VMEM((rows, cin), bf),
+            pltpu.VMEM((rows, cin), bf),
             pltpu.VMEM((LEVELS, rows, 256), bf),
             pltpu.VMEM((LEVELS, rows, 256), bf),
             pltpu.VMEM((LEVELS, rows, 128), bf),
@@ -200,6 +213,7 @@
             pltpu.VMEM((LEVELS - 1, rows, 256), bf),
             pltpu.VMEM((LEVELS, rows, 256), bf),
             pltpu.VMEM((cin, width), bf),
+            dma((3,)),
             dma,
             dma((LEVELS,)),
             dma((LEVELS,)),
@@ -211,7 +225,7 @@
             dma((LEVELS,)),
         ],
         compiler_params=pltpu.CompilerParams(
-            collective_id=0, has_side_effects=True, vmem_limit_bytes=48 * 2**20
+            collective_id=0, has_side_effects=True, vmem_limit_bytes=63 * 2**20
         ),
         name="attention",
     )(query_in, key_in, value_in, length, out_weight)

time: 34.8 us -> 31.9 us (0.917)
  local copies, waits for them, and re-layouts: 5.06 us -> 1.65 us
  Pallas kernels: 28.9 us -> 29.5 us
    unnamed x9 -> x1, local copies, waits for them, and re-layouts: 5.06 us -> 1.65 us
    pallas_call x1, Pallas kernels: 28.9 us -> 29.5 us  [body(): pl.pallas_call(functools.partial(kernel, n), out_shape=jax.ShapeDtypeStru...]
where the time goes in v2:
time: 31.9 us; the launch traced here: 31.8 us
  Pallas kernels  29.5 us (92%)
  local copies, waits for them, and re-layouts  1.65 us (5%)
  between operations  0.66 us (2%)
    pallas_call x1, Pallas kernels, body(): pl.pallas_call(functools.partial(kernel, n), out_shape=jax.ShapeDtypeStru...  29.5 us
    unnamed x1, local copies, waits for them, and re-layouts  1.65 us

profile of v2, /device:TPU:0, one launch (start us, length us, event | category | flops | bytes accessed | tf_op | source)
XLA Modules:
  0.0 31.8 jit_solution(8618604664097297877)
XLA Ops:
  0.7 29.5 %attention.1 = bf16[80,1536]{1,0:T(8,128)(2,1)} custom-call(bf16[80,768]{1,0:T(8,128)(2,1)} %q_hbm.1, bf16[80,768]{1,0:T(8,128)(2,1)} %k_hbm.1, bf16[80,768]{1,0:T(8,128)(2,1)} %v_hbm.1, s32[1]{0:T(128)S(6)} %copy.7.len_ref, bf16[768,1536]{1,0:T(8,128)(2,1)} %w_hbm.1), custom_call_target="tpu_custom_call" | custom-call | tf_op jit(solution)/shard_map/attention/pallas_call | solution.py:198
  30.1 1.7 %copy.8 = bf16[80,1536]{1,0:T(8,128)(2,1)} copy(bf16[80,1536]{1,0:T(8,128)(2,1)} %attention.1) | data formatting | bytes 491520

commit v3 on v1

v3 whole, which is shorter than its diff:
```python
import functools

import jax
import jax.numpy as jnp
from jax import lax
from jax.experimental import pallas as pl
from jax.experimental.pallas import tpu as pltpu
from jax.sharding import PartitionSpec as P

HEADS = 12
HDIM = 64
LEVELS = 4
PAIRS = 2 * LEVELS * HDIM
MESH = pl.DeviceIdType.MESH
NT = (((1,), (1,)), ((), ()))
F32 = jnp.float32
BF16 = jnp.bfloat16
FAR_FIRST = (2, 1, 3)


def kernel(
    n, q_hbm, k_hbm, v_hbm, len_hbm, w_hbm, out_ref,
    len_ref, q_in, k_in, v_in, kv2, kv1, q2, q1, kv1_send, q1_send, o2, o1, o2_send, o1_send, w_buf,
    in_sem, own_sem, w_sem,
    one_send, kv2_recv, hop2_recv, hop2_send, kv1_recv, hop1_send, q2_recv, q1_recv, o2_recv, o1_recv,
):
    rows = out_ref.shape[0]
    half = rows // 2
    cols = n // LEVELS
    chips = cols // 2
    me = lax.axis_index("ctx")
    level, col = me // cols, me % cols
    core = col % 2
    flip = 1 - 2 * core
    sibling = me + flip
    low = lax.broadcasted_iota(jnp.int32, (1, 2 * HDIM), 1) < HDIM

    def up(off):
        return (level + off) % LEVELS

    def source(off):
        return (level + LEVELS - off) % LEVELS

    def chip_col(off):
        return (col + 2 * off) % cols

    def pair(ref, g):
        return ref.at[:, pl.ds(pl.multiple_of(g * 2 * HDIM, 2 * HDIM), 2 * HDIM)]

    local = [
        pltpu.make_async_copy(hbm.at[:, pl.ds(PAIRS, LEVELS * HDIM)], ref, in_sem.at[i])
        for i, (hbm, ref) in enumerate(((k_hbm, k_in), (v_hbm, v_in), (q_hbm, q_in)))
    ]
    own = [
        pltpu.make_async_copy(pair(k_hbm, level), kv2.at[me, 0], own_sem.at[0]),
        pltpu.make_async_copy(pair(v_hbm, level), kv2.at[me, 1], own_sem.at[1]),
        pltpu.make_async_copy(pair(q_hbm, level), q2.at[level], own_sem.at[2]),
        pltpu.make_async_copy(len_hbm, len_ref, own_sem.at[3]),
    ]
    w_copy = pltpu.make_async_copy(w_hbm, w_buf, w_sem)
    for copy in local + own:
        copy.start()

    barrier = pltpu.get_barrier_semaphore()
    greeted = [up(off) * cols + col for off in range(1, LEVELS)] + [sibling]
    greeted += [level * cols + chip_col(off) for off in range(1, chips)]
    for other in greeted:
        pl.semaphore_signal(barrier, inc=1, device_id={"ctx": other}, device_id_type=MESH)

    for copy in local:
        copy.wait()
    for g in range(LEVELS):
        one = slice(HDIM * g, HDIM * g + HDIM)
        kv1_send[g] = jnp.concatenate([k_in[:, one], v_in[:, one]], axis=1)
        q_one = q_in[:, one].astype(F32)
        q1_send[g] = jnp.concatenate([q_one[:half], q_one[half:]], axis=1).astype(BF16)
    kv1[me] = kv1_send[level]
    q1[level] = q1_send[level]

    pl.semaphore_wait(barrier, len(greeted))

    sent = []

    def remote(src, dst, send_sem, recv_sem, target):
        copy = pltpu.make_async_remote_copy(
            src_ref=src, dst_ref=dst, send_sem=send_sem, recv_sem=recv_sem,
            device_id={"ctx": target}, device_id_type=MESH,
        )
        copy.start()
        sent.append(copy)

    def arrived(buf, sem):
        pltpu.make_async_remote_copy(
            src_ref=buf, dst_ref=buf, send_sem=sem, recv_sem=sem,
            device_id={"ctx": sibling}, device_id_type=MESH,
        ).wait_recv()

    def send(src, dst, kind, off, recv_sem):
        remote(src, dst, one_send.at[kind, off], recv_sem, up(off) * cols + col)

    def send_pair(off):
        send(pair(k_hbm, up(off)), kv2.at[me, 0], 0, off, kv2_recv.at[level, 0])
        send(pair(v_hbm, up(off)), kv2.at[me, 1], 1, off, kv2_recv.at[level, 1])
        send(pair(q_hbm, up(off)), q2.at[level], 2, off, q2_recv.at[level])

    def send_single(off):
        send(kv1_send.at[up(off)], kv1.at[me], 3, off, kv1_recv.at[me])
        send(q1_send.at[up(off)], q1.at[level], 4, off, q1_recv.at[level])

    used = [0, 0]
    stages = ((kv2, hop2_send, hop2_recv), (kv1, hop1_send, kv1_recv))

    def forward(stage, slot, target):
        buf, send_sem, recv_sem = stages[stage]
        remote(buf.at[slot], buf.at[slot], send_sem.at[used[stage]], recv_sem.at[slot], target)
        used[stage] += 1

    def spread(stage, slot):
        for off in range(1, chips):
            forward(stage, slot, level * cols + chip_col(off))
        forward(stage, slot, sibling)

    def from_column(stage, off):
        slot = source(off) * cols + col
        if stage == 0:
            arrived(kv2.at[slot, 0], kv2_recv.at[source(off), 0])
            arrived(kv2.at[slot, 1], kv2_recv.at[source(off), 1])
        else:
            arrived(kv1.at[slot], kv1_recv.at[slot])
        spread(stage, slot)

    def from_chips(stage):
        buf, _, recv_sem = stages[stage]
        for off in (0,) + FAR_FIRST:
            for hop in range(1, chips):
                slot = source(off) * cols + chip_col(hop)
                arrived(buf.at[slot], recv_sem.at[slot])
                forward(stage, slot, sibling)

    def from_sibling(stage):
        buf, _, recv_sem = stages[stage]
        for off in (0,) + FAR_FIRST:
            for hop in range(chips):
                slot = source(off) * cols + chip_col(hop) + flip
                arrived(buf.at[slot], recv_sem.at[slot])

    for off in FAR_FIRST:
        send_pair(off)
    for copy in own:
        copy.wait()
    w_copy.start()
    spread(0, me)
    spread(1, me)
    for off in FAR_FIRST:
        send_single(off)
    for off in FAR_FIRST:
        from_column(0, off)
    for off in FAR_FIRST:
        from_column(1, off)
    from_chips(0)
    from_sibling(0)

    valid = len_ref[0]
    frames = n * rows
    scale = jnp.asarray(HDIM ** -0.5, BF16)
    live = lax.broadcasted_iota(jnp.int32, (1, frames), 1) < valid

    def attend(q, k, v):
        s = lax.dot_general(q, k, NT, preferred_element_type=F32)
        s = jnp.where(live, s, F32(-1e30))
        e = jnp.exp(s - jnp.max(s, axis=1, keepdims=True))
        total = jnp.sum(e, axis=1, keepdims=True)
        return jnp.dot(e.astype(BF16), v, preferred_element_type=F32) / total

    def keep(j, out):
        row = (j * cols + col) * rows + lax.broadcasted_iota(jnp.int32, (rows, 1), 0)
        return jnp.where(row < valid, out, F32(0.0))

    def attend_pair(off):
        j = up(off)
        if off:
            arrived(q2.at[j], q2_recv.at[j])
        q = q2[j] * scale
        zero = jnp.zeros_like(q)
        q = jnp.concatenate([jnp.where(low, q, zero), jnp.where(low, zero, q)], axis=0)
        out = attend(q, kv2[:, 0].reshape(frames, 2 * HDIM), kv2[:, 1].reshape(frames, 2 * HDIM))
        out = keep(j, jnp.where(low, out[:rows], out[rows:])).astype(BF16)
        if off:
            o2_send[off] = out
            send(o2_send.at[off], o2.at[level], 5, off, o2_recv.at[level])
        else:
            o2[level] = out

    def attend_single(off):
        j = up(off)
        if off:
            arrived(q1.at[j], q1_recv.at[j])
        q = q1[j].astype(F32)
        zero = jnp.zeros_like(q)
        q = jnp.concatenate(
            [jnp.where(low, q, zero), jnp.where(low, pltpu.roll(q, HDIM, 1), zero)], axis=0
        ).astype(BF16) * scale
        kv = kv1[...].reshape(frames, 2 * HDIM)
        out = keep(j, attend(q, kv, kv))
        out = jnp.where(low, pltpu.roll(out[half:], HDIM, 1), out[:half]).astype(BF16)
        if off:
            o1_send[off] = out
            send(o1_send.at[off], o1.at[level], 6, off, o1_recv.at[level])
        else:
            o1[level] = out

    attend_pair(FAR_FIRST[0])
    attend_pair(FAR_FIRST[1])
    from_chips(1)
    attend_pair(FAR_FIRST[2])
    attend_pair(0)
    from_sibling(1)
    for off in FAR_FIRST + (0,):
        attend_single(off)

    w_copy.wait()
    for off in FAR_FIRST:
        arrived(o2.at[source(off)], o2_recv.at[source(off)])
    pairs = jnp.concatenate([o2[g] for g in range(LEVELS)], axis=1)
    total = jnp.dot(pairs, w_buf[:PAIRS, :], preferred_element_type=F32)
    for off in FAR_FIRST:
        arrived(o1.at[source(off)], o1_recv.at[source(off)])
    parts = []
    for g in range(0, LEVELS, 2):
        even, odd = o1[g].astype(F32), o1[g + 1].astype(F32)
        top = jnp.where(low, pltpu.roll(even, HDIM, 1), odd)
        bottom = jnp.where(low, even, pltpu.roll(odd, HDIM, 1))
        parts.append(jnp.concatenate([top, bottom], axis=0).astype(BF16))
    singles = jnp.concatenate(parts, axis=1)
    total = total + jnp.dot(singles, w_buf[PAIRS:, :], preferred_element_type=F32)
    out_ref[...] = total.astype(BF16)
    for copy in sent:
        copy.wait_send()


def body(n, query_in, key_in, value_in, length, out_weight):
    rows, cin = query_in.shape
    width = out_weight.shape[1]
    chips = n // LEVELS // 2
    hops = LEVELS * chips + LEVELS * (chips - 1)
    lanes = 2 * HDIM
    dma = pltpu.SemaphoreType.DMA
    hbm = pl.BlockSpec(memory_space=pl.ANY)

    def vmem(*shape):
        return pltpu.VMEM(shape, BF16)

    return pl.pallas_call(
        functools.partial(kernel, n),
        out_shape=jax.ShapeDtypeStruct((rows, width), BF16),
        in_specs=[hbm] * 5,
        out_specs=pl.BlockSpec(memory_space=pltpu.VMEM),
        scratch_shapes=[
            pltpu.SMEM((1,), jnp.int32),
            vmem(rows, LEVELS * HDIM),
            vmem(rows, LEVELS * HDIM),
            vmem(rows, LEVELS * HDIM),
            vmem(n, 2, rows, lanes),
            vmem(n, rows, lanes),
            vmem(LEVELS, rows, lanes),
            vmem(LEVELS, rows // 2, lanes),
            vmem(LEVELS, rows, lanes),
            vmem(LEVELS, rows // 2, lanes),
            vmem(LEVELS, rows, lanes),
            vmem(LEVELS, rows // 2, lanes),
            vmem(LEVELS, rows, lanes),
            vmem(LEVELS, rows // 2, lanes),
            vmem(cin, width),
            dma((3,)),
            dma((4,)),
            dma,
            dma((7, LEVELS)),
            dma((LEVELS, 2)),
            dma((n,)),
            dma((hops,)),
            dma((n,)),
            dma((hops,)),
            dma((LEVELS,)),
            dma((LEVELS,)),
            dma((LEVELS,)),
            dma((LEVELS,)),
        ],
        compiler_params=pltpu.CompilerParams(
            collective_id=0, has_side_effects=True, vmem_limit_bytes=63 * 2**20
        ),
        name="attention",
    )(query_in, key_in, value_in, length, out_weight)


def solution(mesh):
    split = P(("grp", "ctx"), None)
    return jax.shard_map(
        functools.partial(body, mesh.shape["ctx"]),
        mesh=mesh,
        in_specs=(split, split, split, P("grp"), P()),
        out_specs=split,
        check_vma=False,
    )
```

time: 34.8 us -> 29.4 us (0.84)
  local copies, waits for them, and re-layouts: 5.06 us -> 1.65 us
  Pallas kernels: 28.9 us -> 26.8 us
    unnamed x9 -> x1, local copies, waits for them, and re-layouts: 5.06 us -> 1.65 us
    pallas_call x1, Pallas kernels: 28.9 us -> 26.8 us  [body(): pl.pallas_call(functools.partial(kernel, n), out_shape=jax.ShapeDtypeStru...]
where the time goes in v3:
time: 29.4 us; the launch traced here: 29.2 us
  Pallas kernels  26.8 us (91%)
  local copies, waits for them, and re-layouts  1.65 us (6%)
  between operations  0.66 us (2%)
    pallas_call x1, Pallas kernels, body(): pl.pallas_call(functools.partial(kernel, n), out_shape=jax.ShapeDtypeStru...  26.8 us
    unnamed x1, local copies, waits for them, and re-layouts  1.65 us

profile of v3, /device:TPU:0, one launch (start us, length us, event | category | flops | bytes accessed | tf_op | source)
XLA Modules:
  0.0 29.2 jit_solution(6432731633738900428)
XLA Ops:
  0.7 26.8 %attention.1 = bf16[80,1536]{1,0:T(8,128)(2,1)} custom-call(bf16[80,768]{1,0:T(8,128)(2,1)} %q_hbm.1, bf16[80,768]{1,0:T(8,128)(2,1)} %k_hbm.1, bf16[80,768]{1,0:T(8,128)(2,1)} %v_hbm.1, s32[1]{0:T(128)S(6)} %copy.7.len_hbm, bf16[768,1536]{1,0:T(8,128)(2,1)} %w_hbm.1), custom_call_target="tpu_custom_call" | custom-call | tf_op jit(solution)/shard_map/attention/pallas_call | solution.py:253
  27.5 1.7 %copy.8 = bf16[80,1536]{1,0:T(8,128)(2,1)} copy(bf16[80,1536]{1,0:T(8,128)(2,1)} %attention.1) | data formatting | bytes 491520

commit v4 on v3

--- a/solution.py
+++ b/solution.py
@@ -252,7 +252,7 @@
 
     return pl.pallas_call(
         functools.partial(kernel, n),
-        out_shape=jax.ShapeDtypeStruct((rows, width), BF16),
+        out_shape=pltpu.VMEM((rows, width), BF16),
         in_specs=[hbm] * 5,
         out_specs=pl.BlockSpec(memory_space=pltpu.VMEM),
         scratch_shapes=[

time: 29.4 us -> 27.7 us (0.942)
  local copies, waits for them, and re-layouts: 1.65 us -> 0.7 us
  Pallas kernels: 26.8 us -> 26.2 us
    unnamed x1, local copies, waits for them, and re-layouts: 1.65 us -> 0.7 us
    pallas_call x1, Pallas kernels: 26.8 us -> 26.2 us  [body(): pl.pallas_call(functools.partial(kernel, n), out_shape=pltpu.VMEM((rows,...]
where the time goes in v4:
time: 27.7 us; the launch traced here: 27.5 us
  Pallas kernels  26.2 us (95%)
  local copies, waits for them, and re-layouts  0.7 us (3%)
  between operations  0.66 us (2%)
    pallas_call x1, Pallas kernels, body(): pl.pallas_call(functools.partial(kernel, n), out_shape=pltpu.VMEM((rows,...  26.2 us
    unnamed x1, local copies, waits for them, and re-layouts  0.7 us

profile of v4, /device:TPU:0, one launch (start us, length us, event | category | flops | bytes accessed | tf_op | source)
XLA Modules:
  0.0 27.5 jit_solution(5224767249913022154)
XLA Ops:
  0.7 26.2 %attention.1 = bf16[80,1536]{1,0:T(8,128)(2,1)S(1)} custom-call(bf16[80,768]{1,0:T(8,128)(2,1)} %q_hbm.1, bf16[80,768]{1,0:T(8,128)(2,1)} %k_hbm.1, bf16[80,768]{1,0:T(8,128)(2,1)} %v_hbm.1, s32[1]{0:T(128)S(6)} %copy.8.len_hbm, bf16[768,1536]{1,0:T(8,128)(2,1)} %w_hbm.1), custom_call_target="tpu_custom_call" | custom-call | tf_op jit(solution)/shard_map/attention/pallas_call | solution.py:253
  26.8 0.7 %copy.7 = bf16[80,1536]{1,0:T(8,128)(2,1)} copy(bf16[80,1536]{1,0:T(8,128)(2,1)S(1)} %attention.1) | data formatting | bytes 491520

commit v5 on v4

--- a/solution.py
+++ b/solution.py
@@ -148,7 +148,6 @@
         send_pair(off)
     for copy in own:
         copy.wait()
-    w_copy.start()
     spread(0, me)
     spread(1, me)
     for off in FAR_FIRST:
@@ -157,6 +156,7 @@
         from_column(0, off)
     for off in FAR_FIRST:
         from_column(1, off)
+    w_copy.start()
     from_chips(0)
     from_sibling(0)
 

time: 27.7 us -> 27.7 us (level)
  no operation moved by 1% of the time
where the time goes in v5:
time: 27.7 us; the launch traced here: 27.5 us
  Pallas kernels  26.2 us (95%)
  local copies, waits for them, and re-layouts  0.7 us (3%)
  between operations  0.66 us (2%)
    pallas_call x1, Pallas kernels, body(): pl.pallas_call(functools.partial(kernel, n), out_shape=pltpu.VMEM((rows,...  26.2 us
    unnamed x1, local copies, waits for them, and re-layouts  0.7 us

profile of v5, /device:TPU:0, one launch (start us, length us, event | category | flops | bytes accessed | tf_op | source)
XLA Modules:
  0.0 27.5 jit_solution(16233766951456692587)
XLA Ops:
  0.7 26.2 %attention.1 = bf16[80,1536]{1,0:T(8,128)(2,1)S(1)} custom-call(bf16[80,768]{1,0:T(8,128)(2,1)} %q_hbm.1, bf16[80,768]{1,0:T(8,128)(2,1)} %k_hbm.1, bf16[80,768]{1,0:T(8,128)(2,1)} %v_hbm.1, s32[1]{0:T(128)S(6)} %copy.8.len_hbm, bf16[768,1536]{1,0:T(8,128)(2,1)} %w_hbm.1), custom_call_target="tpu_custom_call" | custom-call | tf_op jit(solution)/shard_map/attention/pallas_call | solution.py:253
  26.8 0.7 %copy.7 = bf16[80,1536]{1,0:T(8,128)(2,1)} copy(bf16[80,1536]{1,0:T(8,128)(2,1)S(1)} %attention.1) | data formatting | bytes 491520
